TPU v7x, 128 devices: a whole 4x4x4 slice. The times are simulated.
128 devices in a mesh: slab: 16 (over x, y_hi, core), tile: 8 (over y_lo, z).
Axes of the slice: x: 4, y: 4 (y_hi: 2, y_lo: 2; y = y_hi * 2 + y_lo), z: 4, core: 2. Of those that a mesh axis runs over, the one named last changes fastest.
Arguments:
- velocity: float32 [3, 512, 128, 128], P(None, 'slab', 'tile'), may hold values from -4 to 4
- viscosity: float32 [512, 128, 128], P('slab', 'tile'), may hold values from 0.2 to 0.6
- basis: bfloat16 [32, 3, 512, 128, 128], P(None, None, ('slab', 'tile')), may hold values from -6 to 6
- sigma: float32 [32], replicated, may hold values from 0.3 to 3
- rotation: float32 [35, 32], replicated, may hold values from -1 to 1
Outputs:
- advanced: float32 [3, 512, 128, 128], P(None, 'slab', 'tile')
- r_factor: float32 [35, 35], replicated
- new_basis: bfloat16 [32, 3, 512, 128, 128], P(None, None, ('slab', 'tile'))
All inputs are finite; a program needn't handle non-finite values.
Results may differ from a plain program's by a relative error of at most 0.001.
Values sent between devices are 32-bit elements; how exact they have to be, the bound alone decides.
A program may use at most 256 MiB of HBM per device.

v0:
```python
import math
import jax
import jax.numpy as jnp
from jax import lax
from jax.sharding import PartitionSpec as P

step_size = 0.25


def extended(block, sides, width):
    for axis, dim in sides:
        count = lax.axis_size(axis)
        forward = [(i, i + 1) for i in range(count - 1)]
        forward.append((count - 1, 0))
        backward = [(target, source) for source, target in forward]
        low = lax.ppermute(
            lax.slice_in_dim(block, block.shape[dim] - width, None, axis=dim), axis, forward
        )
        high = lax.ppermute(lax.slice_in_dim(block, 0, width, axis=dim), axis, backward)
        block = jnp.concatenate([low, block, high], axis=dim)
    return block


def upper_factor(gram):
    order = gram.shape[0]
    positions = jnp.arange(order)
    factor = jnp.zeros_like(gram)
    for column_index in range(order):
        above = factor[:, column_index]
        remainder = gram[column_index] - jnp.dot(
            above, factor, precision=lax.Precision.HIGHEST, preferred_element_type=jnp.float32
        )
        pivot = jnp.sqrt(remainder[column_index])
        new_row = jnp.where(positions >= column_index, remainder / pivot, 0.0)
        factor = factor.at[column_index].set(new_row)
    return factor


def upper_solve(factor, right_hand):
    order = factor.shape[0]
    solved = jnp.zeros_like(right_hand)
    for row_index in range(order - 1, -1, -1):
        partial_sum = jnp.dot(
            factor[row_index],
            solved,
            precision=lax.Precision.HIGHEST,
            preferred_element_type=jnp.float32,
        )
        solved = solved.at[row_index].set(
            (right_hand[row_index] - partial_sum) / factor[row_index, row_index]
        )
    return solved


def advance(padded, viscosity):
    centre = padded[:, 1:-1, 1:-1, :]
    forward_x = padded[:, 2:, 1:-1, :]
    backward_x = padded[:, :-2, 1:-1, :]
    forward_z = padded[:, 1:-1, 2:, :]
    backward_z = padded[:, 1:-1, :-2, :]
    walled = jnp.pad(centre, ((0, 0), (0, 0), (0, 0), (1, 1)))
    above_y = walled[..., 2:]
    below_y = walled[..., :-2]
    laplace = forward_x + backward_x + forward_z + backward_z + above_y + below_y - 6.0 * centre
    carried = (
        centre[0:1] * (forward_x - backward_x)
        + centre[1:2] * (above_y - below_y)
        + centre[2:3] * (forward_z - backward_z)
    )
    return centre + step_size * (viscosity * laplace - 0.5 * carried)


def shards(velocity, viscosity, basis, sigma, rotation):
    current = velocity
    history = [velocity]
    for repeat in range(2):
        padded = extended(current, (("slab", 1), ("tile", 2)), 1)
        current = advance(padded, viscosity)
        history.append(current)
    snapshots = lax.all_to_all(jnp.stack(history), "tile", split_axis=2, concat_axis=3, tiled=True)
    strip_width = basis.shape[2]
    row_count = (
        3
        * strip_width
        * lax.axis_size("slab")
        * lax.axis_size("tile")
        * basis.shape[3]
        * basis.shape[4]
    )
    row_scale = math.sqrt(row_count)
    width_all = sigma.shape[0] + 3
    scaled = basis.astype(jnp.float32) * sigma[:, None, None, None, None]
    columns = jnp.concatenate([scaled, snapshots], 0).reshape(width_all, -1)
    local_gram = jnp.dot(
        columns, columns.T, precision=lax.Precision.HIGHEST, preferred_element_type=jnp.float32
    )
    gram = lax.psum(local_gram, ("slab", "tile"))
    factor = upper_factor(gram)
    mixing = upper_solve(factor, rotation) * row_scale
    rotated = jnp.dot(
        mixing.T, columns, precision=lax.Precision.HIGHEST, preferred_element_type=jnp.float32
    )
    rotated = rotated.reshape(basis.shape).astype(jnp.bfloat16)
    return (current, factor / row_scale, rotated)


def solution(mesh):
    in_specs = (
        P(None, "slab", "tile", None),
        P("slab", "tile", None),
        P(None, None, ("slab", "tile"), None, None),
        P(),
        P(),
    )
    out_specs = (P(None, "slab", "tile", None), P(), P(None, None, ("slab", "tile"), None, None))
    return jax.shard_map(shards, mesh=mesh, in_specs=in_specs, out_specs=out_specs, check_vma=False)
```

profile of v0, /device:TPU:1, one launch (start us, length us, event | category | flops | bytes accessed | tf_op | source)
XLA Modules:
  0.0 461.0 jit_solution(1416673244914366114)
XLA Ops:
  1.4 4.3 collective-permute-start.1
  7.9 2.6 collective-permute-done
  10.5 3.9 collective-permute-start.2
  16.8 2.7 collective-permute-done.3
  19.6 1.8 multiply_add_fusion.1
  21.4 3.4 collective-permute-start.5
  25.7 4.1 collective-permute-done.4
  30.0 1.5 collective-permute-start.7
  31.5 1.4 collective-permute-done.6
  32.9 2.2 collective-permute-done.7
  35.1 1.8 fusion.306
  36.9 1.6 pad_maximum_fusion.1
  38.6 3.8 all-to-all-start
  42.4 11.8 %convert_multiply_fusion = f32[32,3,4,128,128]{4,0,3,2,1:T(8,128)S(1)} fusion(bf16[32,3,4,128,128]{4,3,2,1,0:T(8,128)(2,1)} %param.147, f32[32]{0:T(128)} %param.148), kind=kLoop, calls=%fused_computation.8 | loop fusion | flops 12582912 | bytes 37748864 | tf_op jit(solution)/shard_map/mul | solution.py:92
  54.1 28.1 %copy.82 = f32[32,3,4,128,128]{4,3,2,1,0:T(8,128)} copy(f32[32,3,4,128,128]{4,0,3,2,1:T(8,128)S(1)} %convert_multiply_fusion) | data formatting | bytes 50331648 | tf_op jit(solution)/shard_map/mul | solution.py:92
  82.3 25.1 %copy.100 = f32[4,8,1536,128]{3,1,2,0:T(8,128)} copy(f32[4,8,1536,128]{3,2,1,0:T(8,128)} %bitcast.1128) | data formatting | bytes 50331648
  111.6 1.4 copy-done.3
  113.0 3.0 copy.46
  116.0 28.8 %fusion.9 = f32[35,35]{1,0:T(8,128)S(1)} fusion(f32[3,3,4,128,128]{4,0,3,2,1:T(4,128)S(1)} %bitcast.1130, f32[32,3,4,128,128]{4,0,3,2,1:T(8,128)} %copy-done.1), kind=kOutput, calls=%fused_computation.15 | convolution fusion | flops 2897018880 | bytes 27530020 | tf_op jit(solution)/shard_map/dot_general | solution.py:94
  144.8 68.9 %psum.7 = f32[35,35]{1,0:T(8,128)S(1)} all-reduce(f32[35,35]{1,0:T(8,128)S(1)} %fusion.9), channel_id=1, replica_groups=mesh['slab'=16,'tile'=8] {'slab','tile'}, use_global_device_ids=true, to_apply=%region_0.1 | all-reduce | flops 1225 | bytes 9800 | tf_op jit(solution)/shard_map/psum | solution.py:97
  298.0 1.4 fusion.87
  299.7 1.5 fusion.89
  303.0 1.4 fusion.93
  304.7 1.4 fusion.95
  306.4 1.4 fusion.97
  308.1 1.5 fusion.99
  309.9 1.4 fusion.101
  313.2 1.5 fusion.105
  316.6 1.5 fusion.109
  318.3 1.4 fusion.111
  320.0 1.4 fusion.113
  323.3 1.5 fusion.117
  326.7 1.4 fusion.121
  331.7 1.5 fusion.127
  333.4 1.5 fusion.129
  335.2 1.4 fusion.131
  336.8 1.5 fusion.133
  338.6 1.4 fusion.135
  340.3 1.4 fusion.137
  342.0 1.4 fusion.139
  345.3 1.5 fusion.143
  348.6 1.4 fusion.147
  352.0 1.4 fusion.151
  353.6 10.1 %pad_maximum_fusion = f32[35,196608]{1,0:T(8,128)S(1)} fusion(f32[3,196608]{1,0:T(4,128)S(1)} %bitcast.1131, f32[32,196608]{1,0:T(8,128)} %bitcast.1127), kind=kLoop, calls=%fused_computation.4 | loop fusion | flops 6881280 | bytes 55050240 | tf_op jit(solution)/shard_map/concatenate | solution.py:93
  363.7 14.4 %copy.89 = f32[5,8,1536,128]{3,2,1,0:T(8,128)} copy(f32[5,8,1536,128]{3,1,2,0:T(8,128)S(1)} %bitcast.1125) | data formatting | bytes 62914560
  378.1 20.3 %slice.2142 = f32[35,1536,128]{2,1,0:T(8,128)} slice(f32[40,1536,128]{2,1,0:T(8,128)} %bitcast.1126), slice={[0:35], [0:1536], [0:128]} | slice | bytes 55050240
  398.3 48.0 %fusion.6 = bf16[32,3,4,128,128]{4,0,3,2,1:T(8,128)(2,1)S(1)} fusion(f32[3,4,128,128,35]{3,2,1,0,4:T(8,128)} %bitcast.1124, f32[35,32]{0,1:T(8,128)S(1)} %scatter.349), kind=kOutput, calls=%fused_computation.9 | convolution fusion | flops 2648704000 | bytes 40112512 | tf_op jit(solution)/shard_map/dot_general | solution.py:100
  446.4 14.5 %copy.85 = bf16[32,3,4,128,128]{4,3,2,1,0:T(8,128)(2,1)} copy(bf16[32,3,4,128,128]{4,0,3,2,1:T(8,128)(2,1)S(1)} %fusion.6) | data formatting | bytes 25165824
  (352 shorter events, 92.3 us)
Async XLA Ops:
  1.4 5.3 %collective-permute-start.1 = (f32[3,1,16,128]{3,2,0,1:T(8,128)S(1)}, f32[3,1,16,128]{3,2,0,1:T(8,128)S(1)}, u32[]{:S(2)}, u32[]{:S(2)}) collective-permute-start(f32[3,1,16,128]{3,2,0,1:T(8,128)S(1)} %get-tuple-element.905), channel_id=1, source_target_pairs={{0,8},{8,16},{16,24},{24,32},{32,40},{40,48},{48,56},{56,64},{64,7... | collective-permute-start | bytes 73736 | tf_op jit(solution)/shard_map/ppermute | solution.py:16
  5.7 4.8 %collective-permute-start = (f32[3,1,16,128]{3,2,0,1:T(8,128)S(1)}, f32[3,1,16,128]{3,2,0,1:T(8,128)S(1)}, u32[]{:S(2)}, u32[]{:S(2)}) collective-permute-start(f32[3,1,16,128]{3,2,0,1:T(8,128)S(1)} %get-tuple-element.904), channel_id=1, source_target_pairs={{8,0},{16,8},{24,16},{32,24},{40,32},{48,40},{56,48},{64,56},{72,6... | collective-permute-start | bytes 73736 | tf_op jit(solution)/shard_map/ppermute | solution.py:19
  10.5 6.3 %collective-permute-start.2 = (f32[3,34,1,128]{3,2,0,1:T(1,128)S(1)}, f32[3,34,1,128]{3,2,0,1:T(1,128)S(1)}, u32[]{:S(2)}, u32[]{:S(2)}) collective-permute-start(f32[3,34,1,128]{3,2,0,1:T(1,128)S(1)} %get-tuple-element.892), channel_id=1, source_target_pairs={{1,0},{2,1},{3,2},{4,3},{5,4},{6,5},{7,6},{0,7},{9,8},{10,9},{11,1... | collective-permute-start | bytes 156680 | tf_op jit(solution)/shard_map/ppermute | solution.py:19
  14.5 5.1 %collective-permute-start.3 = (f32[3,34,1,128]{3,2,0,1:T(1,128)S(1)}, f32[3,34,1,128]{3,2,0,1:T(1,128)S(1)}, u32[]{:S(2)}, u32[]{:S(2)}) collective-permute-start(f32[3,34,1,128]{3,2,0,1:T(1,128)S(1)} %get-tuple-element.893), channel_id=1, source_target_pairs={{0,1},{1,2},{2,3},{3,4},{4,5},{5,6},{6,7},{7,0},{8,9},{9,10},{10,1... | collective-permute-start | bytes 156680 | tf_op jit(solution)/shard_map/ppermute | solution.py:16
  21.4 4.3 collective-permute-start.5
  24.8 5.1 %collective-permute-start.4 = (f32[3,1,16,128]{3,2,0,1:T(8,128)S(1)}, f32[3,1,16,128]{3,2,0,1:T(8,128)S(1)}, u32[]{:S(2)}, u32[]{:S(2)}) collective-permute-start(f32[3,1,16,128]{3,2,0,1:T(8,128)S(1)} %get-tuple-element.900), channel_id=1, source_target_pairs={{8,0},{16,8},{24,16},{32,24},{40,32},{48,40},{56,48},{64,56},{72,6... | collective-permute-start | bytes 73736 | tf_op jit(solution)/shard_map/ppermute | solution.py:19
  29.9 3.0 collective-permute-start.6
  30.0 5.2 %collective-permute-start.7 = (f32[3,34,1,128]{3,2,0,1:T(1,128)S(1)}, f32[3,34,1,128]{3,2,0,1:T(1,128)S(1)}, u32[]{:S(2)}, u32[]{:S(2)}) collective-permute-start(f32[3,34,1,128]{3,2,0,1:T(1,128)S(1)} %get-tuple-element.891), channel_id=1, source_target_pairs={{0,1},{1,2},{2,3},{3,4},{4,5},{5,6},{6,7},{7,0},{8,9},{9,10},{10,1... | collective-permute-start | bytes 156680 | tf_op jit(solution)/shard_map/ppermute | solution.py:16
  31.5 7.0 %copy-start.4 = (f32[32,16,128]{2,1,0:T(8,128)}, f32[32,16,128]{2,1,0:T(8,128)S(1)}, u32[]{:S(2)}) copy-start(f32[32,16,128]{2,1,0:T(8,128)S(1)} %get-tuple-element.897) | copy-start | bytes 786436
  31.5 7.0 %copy-start.6 = (f32[32,16,128]{2,1,0:T(8,128)}, f32[32,16,128]{2,1,0:T(8,128)S(1)}, u32[]{:S(2)}) copy-start(f32[32,16,128]{2,1,0:T(8,128)S(1)} %get-tuple-element.898) | copy-start | bytes 786436
  35.1 3.4 copy-start.10
  38.6 73.0 %all-to-all-start = ((f32[3,3,32,16,128]{4,3,1,0,2:T(8,128)}), f32[3,3,32,16,128]{4,3,1,0,2:T(8,128)S(1)}, u32[]{:S(2)}, u32[]{:S(2)}) async-start(f32[3,3,32,16,128]{4,3,1,0,2:T(8,128)} %pad_maximum_fusion.1), calls=%async_computation | async-start | bytes 4718592 | tf_op jit(solution)/shard_map/all_to_all | solution.py:80
  54.1 28.2 %copy-start.1 = (f32[32,3,4,128,128]{4,0,3,2,1:T(8,128)}, f32[32,3,4,128,128]{4,0,3,2,1:T(8,128)S(1)}, u32[]{:S(2)}) copy-start(f32[32,3,4,128,128]{4,0,3,2,1:T(8,128)S(1)} %convert_multiply_fusion) | copy-start | bytes 75497472
  82.3 25.1 %copy-start.2 = (f32[35,32]{0,1:T(8,128)S(1)}, f32[35,32]{0,1:T(8,128)}, u32[]{:S(2)}) copy-start(f32[35,32]{0,1:T(8,128)} %param.149) | copy-start | bytes 13444
  82.3 27.3 %copy-start.5 = (f32[32,16,128]{2,1,0:T(8,128)S(1)}, f32[32,16,128]{2,1,0:T(8,128)}, u32[]{:S(2)}) copy-start(f32[32,16,128]{2,1,0:T(8,128)} %copy-done.4) | copy-start | bytes 786436
  82.3 27.3 %copy-start.7 = (f32[32,16,128]{2,1,0:T(8,128)S(1)}, f32[32,16,128]{2,1,0:T(8,128)}, u32[]{:S(2)}) copy-start(f32[32,16,128]{2,1,0:T(8,128)} %copy-done.6) | copy-start | bytes 786436
  82.3 27.2 %copy-start.8 = (f32[32,16,128]{2,1,0:T(8,128)S(1)}, f32[32,16,128]{2,1,0:T(8,128)}, u32[]{:S(2)}) copy-start(f32[32,16,128]{2,1,0:T(8,128)} %param.146) | copy-start | bytes 786436
  82.3 27.2 %copy-start.11 = (f32[3,34,1,128]{3,2,0,1:T(1,128)S(1)}, f32[3,34,1,128]{3,2,0,1:T(1,128)}, u32[]{:S(2)}) copy-start(f32[3,34,1,128]{3,2,0,1:T(1,128)} %copy-done.10) | copy-start | bytes 156676
  110.4 185.6 %copy-start.35 = (f32[32]{0:T(128)S(1)}, f32[32]{0:T(128)}, u32[]{:S(2)}) copy-start(f32[32]{0:T(128)} %get-tuple-element.889) | copy-start | bytes 388
  110.4 186.4 %copy-start.30 = (f32[32]{0:T(128)S(1)}, f32[32]{0:T(128)}, u32[]{:S(2)}) copy-start(f32[32]{0:T(128)} %get-tuple-element.888) | copy-start | bytes 388
  110.4 187.5 %copy-start.29 = (f32[32]{0:T(128)S(1)}, f32[32]{0:T(128)}, u32[]{:S(2)}) copy-start(f32[32]{0:T(128)} %get-tuple-element.887) | copy-start | bytes 388
  110.4 189.2 %copy-start.34 = (f32[32]{0:T(128)S(1)}, f32[32]{0:T(128)}, u32[]{:S(2)}) copy-start(f32[32]{0:T(128)} %get-tuple-element.886) | copy-start | bytes 388
  110.5 191.0 %copy-start.28 = (f32[32]{0:T(128)S(1)}, f32[32]{0:T(128)}, u32[]{:S(2)}) copy-start(f32[32]{0:T(128)} %get-tuple-element.885) | copy-start | bytes 388
  110.5 192.6 %copy-start.27 = (f32[32]{0:T(128)S(1)}, f32[32]{0:T(128)}, u32[]{:S(2)}) copy-start(f32[32]{0:T(128)} %get-tuple-element.884) | copy-start | bytes 388
  110.5 194.3 %copy-start.26 = (f32[32]{0:T(128)S(1)}, f32[32]{0:T(128)}, u32[]{:S(2)}) copy-start(f32[32]{0:T(128)} %get-tuple-element.883) | copy-start | bytes 388
  110.5 196.0 %copy-start.25 = (f32[32]{0:T(128)S(1)}, f32[32]{0:T(128)}, u32[]{:S(2)}) copy-start(f32[32]{0:T(128)} %get-tuple-element.882) | copy-start | bytes 388
  110.5 197.6 %copy-start.24 = (f32[32]{0:T(128)S(1)}, f32[32]{0:T(128)}, u32[]{:S(2)}) copy-start(f32[32]{0:T(128)} %get-tuple-element.881) | copy-start | bytes 388
  110.5 199.4 %copy-start.23 = (f32[32]{0:T(128)S(1)}, f32[32]{0:T(128)}, u32[]{:S(2)}) copy-start(f32[32]{0:T(128)} %get-tuple-element.880) | copy-start | bytes 388
  110.5 201.1 %copy-start.22 = (f32[32]{0:T(128)S(1)}, f32[32]{0:T(128)}, u32[]{:S(2)}) copy-start(f32[32]{0:T(128)} %get-tuple-element.879) | copy-start | bytes 388
  110.5 202.7 %copy-start.33 = (f32[32]{0:T(128)S(1)}, f32[32]{0:T(128)}, u32[]{:S(2)}) copy-start(f32[32]{0:T(128)} %get-tuple-element.878) | copy-start | bytes 388
  110.5 204.4 %copy-start.21 = (f32[32]{0:T(128)S(1)}, f32[32]{0:T(128)}, u32[]{:S(2)}) copy-start(f32[32]{0:T(128)} %get-tuple-element.877) | copy-start | bytes 388
  110.5 206.1 %copy-start.20 = (f32[32]{0:T(128)S(1)}, f32[32]{0:T(128)}, u32[]{:S(2)}) copy-start(f32[32]{0:T(128)} %get-tuple-element.876) | copy-start | bytes 388
  110.6 207.8 %copy-start.19 = (f32[32]{0:T(128)S(1)}, f32[32]{0:T(128)}, u32[]{:S(2)}) copy-start(f32[32]{0:T(128)} %get-tuple-element.875) | copy-start | bytes 388
  110.6 209.5 %copy-start.18 = (f32[32]{0:T(128)S(1)}, f32[32]{0:T(128)}, u32[]{:S(2)}) copy-start(f32[32]{0:T(128)} %get-tuple-element.873) | copy-start | bytes 388
  110.6 211.1 %copy-start.17 = (f32[32]{0:T(128)S(1)}, f32[32]{0:T(128)}, u32[]{:S(2)}) copy-start(f32[32]{0:T(128)} %get-tuple-element.872) | copy-start | bytes 388
  110.6 212.8 %copy-start.16 = (f32[32]{0:T(128)S(1)}, f32[32]{0:T(128)}, u32[]{:S(2)}) copy-start(f32[32]{0:T(128)} %get-tuple-element.871) | copy-start | bytes 388
  110.6 214.5 %copy-start.15 = (f32[32]{0:T(128)S(1)}, f32[32]{0:T(128)}, u32[]{:S(2)}) copy-start(f32[32]{0:T(128)} %get-tuple-element.870) | copy-start | bytes 388
  110.6 216.1 %copy-start.32 = (f32[32]{0:T(128)S(1)}, f32[32]{0:T(128)}, u32[]{:S(2)}) copy-start(f32[32]{0:T(128)} %get-tuple-element.869) | copy-start | bytes 388
  110.6 217.8 %copy-start.14 = (f32[32]{0:T(128)S(1)}, f32[32]{0:T(128)}, u32[]{:S(2)}) copy-start(f32[32]{0:T(128)} %get-tuple-element.868) | copy-start | bytes 388
  110.6 219.4 %copy-start.13 = (f32[32]{0:T(128)S(1)}, f32[32]{0:T(128)}, u32[]{:S(2)}) copy-start(f32[32]{0:T(128)} %get-tuple-element.867) | copy-start | bytes 388
  110.6 221.0 %copy-start.12 = (f32[32]{0:T(128)S(1)}, f32[32]{0:T(128)}, u32[]{:S(2)}) copy-start(f32[32]{0:T(128)} %get-tuple-element.866) | copy-start | bytes 388
  110.6 229.6 %copy-start.31 = (f32[32]{0:T(128)S(1)}, f32[32]{0:T(128)}, u32[]{:S(2)}) copy-start(f32[32]{0:T(128)} %get-tuple-element.861) | copy-start | bytes 388
  111.6 1.4 copy-start.3
  213.8 2.1 copy-start.9
  293.9 4.0 copy-start
where the time goes:
time: 469 us; the launch traced here: 461 us
  local copies, waits for them, and re-layouts  153 us (33%)
  matrix products  153 us (33%)
  blocking collectives  68.9 us (15%)
  other arithmetic  28.8 us (6%)
  between operations  25.7 us (5%)
  starting transfers between devices  16.9 us (4%)
  waiting for transfers between devices  14.9 us (3%)
    unnamed x79, local copies, waits for them, and re-layouts  77.9 us
    psum x1, blocking collectives, shards(): gram = lax.psum(local_gram, ('slab', 'tile'))  68.9 us
    dot_general x35, matrix products, upper_solve(): jnp.dot(factor[row_index], solved, precision=lax.Precision.HIGHEST, prefe...  48.9 us
    dot_general x1, matrix products, shards(): jnp.dot(mixing.T, columns, precision=lax.Precision.HIGHEST, preferred_ele...  48 us
    dot_general x1, matrix products, shards(): jnp.dot(columns, columns.T, precision=lax.Precision.HIGHEST, preferred_el...  28.8 us
    mul x1, local copies, waits for them, and re-layouts, shards(): scaled = basis.astype(jnp.float32) * sigma[:, None, None, None, None]  28.1 us
    dot_general x35, matrix products, upper_factor(): jnp.dot(above, factor, precision=lax.Precision.HIGHEST, preferred_element...  27.4 us
    slice x34, local copies, waits for them, and re-layouts, upper_factor(): pivot = jnp.sqrt(remainder[column_index])  20.3 us
  transfers between devices with their start and end apart: 9, of which 7 were waited for; matrix products, arithmetic and copies ran while one was open for 16% of the time, Pallas kernels for 0%

commit v1 on v0

--- a/solution.py
+++ b/solution.py
@@ -94,7 +94,7 @@
     local_gram = jnp.dot(
         columns, columns.T, precision=lax.Precision.HIGHEST, preferred_element_type=jnp.float32
     )
-    gram = lax.psum(local_gram, ("slab", "tile"))
+    gram = jnp.sum(lax.all_gather(local_gram, ("slab", "tile")), axis=0)
     factor = upper_factor(gram)
     mixing = upper_solve(factor, rotation) * row_scale
     rotated = jnp.dot(

time: 469 us -> 754 us (1.61)
  the two profiles are of different devices: /device:TPU:1 before, /device:TPU:0 now
where the time goes in v1:
time: 754 us; the launch traced here: 746 us
  blocking collectives  351 us (47%)
  local copies, waits for them, and re-layouts  153 us (20%)
  matrix products  153 us (20%)
  other arithmetic  30.8 us (4%)
  between operations  25.7 us (3%)
  starting transfers between devices  21.9 us (3%)
  waiting for transfers between devices  11.3 us (1%)
    all_gather x1, blocking collectives, shards(): gram = jnp.sum(lax.all_gather(local_gram, ('slab', 'tile')), axis=0)  351 us
    unnamed x79, local copies, waits for them, and re-layouts  77.9 us
    dot_general x35, matrix products, upper_solve(): jnp.dot(factor[row_index], solved, precision=lax.Precision.HIGHEST, prefe...  48.9 us
    dot_general x1, matrix products, shards(): jnp.dot(mixing.T, columns, precision=lax.Precision.HIGHEST, preferred_ele...  48 us
    dot_general x1, matrix products, shards(): jnp.dot(columns, columns.T, precision=lax.Precision.HIGHEST, preferred_el...  28.8 us
    mul x1, local copies, waits for them, and re-layouts, shards(): scaled = basis.astype(jnp.float32) * sigma[:, None, None, None, None]  28.1 us
    dot_general x35, matrix products, upper_factor(): jnp.dot(above, factor, precision=lax.Precision.HIGHEST, preferred_element...  27.4 us
    slice x34, local copies, waits for them, and re-layouts, upper_factor(): pivot = jnp.sqrt(remainder[column_index])  20.3 us
  transfers between devices with their start and end apart: 9, of which 5 were waited for; matrix products, arithmetic and copies ran while one was open for 10% of the time, Pallas kernels for 0%

profile of v1, /device:TPU:0, one launch (start us, length us, event | category | flops | bytes accessed | tf_op | source)
XLA Modules:
  0.0 746.2 jit_solution(11337266017238637897)
XLA Ops:
  1.4 5.4 collective-permute-start
  6.8 1.5 collective-permute-done.1
  9.6 5.2 collective-permute-start.2
  17.2 3.9 collective-permute-done.3
  21.0 1.8 multiply_add_fusion.1
  23.0 5.3 collective-permute-start.4
  28.3 1.5 collective-permute-done.5
  30.3 1.7 collective-permute-start.7
  32.1 2.0 collective-permute-done.6
  34.1 2.4 collective-permute-done.7
  36.5 1.8 fusion.306
  38.3 1.6 pad_maximum_fusion.1
  39.9 3.8 all-to-all-start
  43.7 11.8 %convert_multiply_fusion = f32[32,3,4,128,128]{4,0,3,2,1:T(8,128)S(1)} fusion(bf16[32,3,4,128,128]{4,3,2,1,0:T(8,128)(2,1)} %param.147, f32[32]{0:T(128)} %param.148), kind=kLoop, calls=%fused_computation.8 | loop fusion | flops 12582912 | bytes 37748864 | tf_op jit(solution)/shard_map/mul | solution.py:92
  55.5 28.1 %copy.82 = f32[32,3,4,128,128]{4,3,2,1,0:T(8,128)} copy(f32[32,3,4,128,128]{4,0,3,2,1:T(8,128)S(1)} %convert_multiply_fusion) | data formatting | bytes 50331648 | tf_op jit(solution)/shard_map/mul | solution.py:92
  83.7 25.1 %copy.100 = f32[4,8,1536,128]{3,1,2,0:T(8,128)} copy(f32[4,8,1536,128]{3,2,1,0:T(8,128)} %bitcast.1130) | data formatting | bytes 50331648
  114.4 3.0 copy.46
  117.4 28.8 %fusion.9 = f32[1,35,35]{2,1,0:T(8,128)S(1)} fusion(f32[3,3,4,128,128]{4,0,3,2,1:T(4,128)S(1)} %bitcast.1132, f32[32,3,4,128,128]{4,0,3,2,1:T(8,128)} %copy-done.1), kind=kOutput, calls=%fused_computation.15 | convolution fusion | flops 2897018880 | bytes 27530020 | tf_op jit(solution)/shard_map/dot_general | solution.py:94
  146.2 350.7 %all-gather.1 = f32[128,35,35]{2,1,0:T(8,128)} all-gather(f32[1,35,35]{2,1,0:T(8,128)S(1)} %fusion.9), channel_id=2, replica_groups=mesh['slab'=16,'tile'=8] {'slab','tile'}, dimensions={0}, use_global_device_ids=true | all-gather | bytes 632100 | tf_op jit(solution)/shard_map/all_gather | solution.py:97
  496.9 2.0 reduce_sum.9
  583.1 1.4 fusion.87
  584.8 1.5 fusion.89
  588.2 1.4 fusion.93
  589.9 1.4 fusion.95
  591.6 1.4 fusion.97
  593.3 1.5 fusion.99
  595.0 1.4 fusion.101
  598.4 1.5 fusion.105
  601.7 1.5 fusion.109
  603.5 1.4 fusion.111
  605.1 1.4 fusion.113
  608.5 1.5 fusion.117
  611.8 1.4 fusion.121
  616.8 1.5 fusion.127
  618.5 1.5 fusion.129
  620.3 1.4 fusion.131
  622.0 1.5 fusion.133
  623.7 1.4 fusion.135
  625.4 1.4 fusion.137
  627.1 1.4 fusion.139
  630.4 1.5 fusion.143
  633.8 1.4 fusion.147
  637.1 1.4 fusion.151
  638.7 10.1 %pad_maximum_fusion = f32[35,196608]{1,0:T(8,128)S(1)} fusion(f32[3,196608]{1,0:T(4,128)S(1)} %bitcast.1133, f32[32,196608]{1,0:T(8,128)} %bitcast.1129), kind=kLoop, calls=%fused_computation.4 | loop fusion | flops 6881280 | bytes 55050240 | tf_op jit(solution)/shard_map/concatenate | solution.py:93
  648.8 14.4 %copy.89 = f32[5,8,1536,128]{3,2,1,0:T(8,128)} copy(f32[5,8,1536,128]{3,1,2,0:T(8,128)S(1)} %bitcast.1127) | data formatting | bytes 62914560
  663.2 20.3 %slice.2142 = f32[35,1536,128]{2,1,0:T(8,128)} slice(f32[40,1536,128]{2,1,0:T(8,128)} %bitcast.1128), slice={[0:35], [0:1536], [0:128]} | slice | bytes 55050240
  683.5 48.0 %fusion.6 = bf16[32,3,4,128,128]{4,0,3,2,1:T(8,128)(2,1)S(1)} fusion(f32[3,4,128,128,35]{3,2,1,0,4:T(8,128)} %bitcast.1126, f32[35,32]{0,1:T(8,128)S(1)} %scatter.349), kind=kOutput, calls=%fused_computation.9 | convolution fusion | flops 2648704000 | bytes 40112512 | tf_op jit(solution)/shard_map/dot_general | solution.py:100
  731.5 14.5 %copy.85 = bf16[32,3,4,128,128]{4,3,2,1,0:T(8,128)(2,1)} copy(bf16[32,3,4,128,128]{4,0,3,2,1:T(8,128)(2,1)S(1)} %fusion.6) | data formatting | bytes 25165824
  (353 shorter events, 92.2 us)
Async XLA Ops:
  1.4 6.9 collective-permute-start.1
  1.4 8.1 %collective-permute-start = (f32[3,1,16,128]{3,2,0,1:T(8,128)S(1)}, f32[3,1,16,128]{3,2,0,1:T(8,128)S(1)}, u32[]{:S(2)}, u32[]{:S(2)}) collective-permute-start(f32[3,1,16,128]{3,2,0,1:T(8,128)S(1)} %get-tuple-element.904), channel_id=1, source_target_pairs={{8,0},{16,8},{24,16},{32,24},{40,32},{48,40},{56,48},{64,56},{72,6... | collective-permute-start | bytes 73736 | tf_op jit(solution)/shard_map/ppermute | solution.py:19
  9.6 7.6 %collective-permute-start.2 = (f32[3,34,1,128]{3,2,0,1:T(1,128)S(1)}, f32[3,34,1,128]{3,2,0,1:T(1,128)S(1)}, u32[]{:S(2)}, u32[]{:S(2)}) collective-permute-start(f32[3,34,1,128]{3,2,0,1:T(1,128)S(1)} %get-tuple-element.892), channel_id=1, source_target_pairs={{1,0},{2,1},{3,2},{4,3},{5,4},{6,5},{7,6},{0,7},{9,8},{10,9},{11,1... | collective-permute-start | bytes 156680 | tf_op jit(solution)/shard_map/ppermute | solution.py:19
  14.8 6.2 collective-permute-start.3
  22.9 6.9 collective-permute-start.5
  23.0 6.9 collective-permute-start.4
  29.9 4.2 collective-permute-start.6
  30.3 6.2 collective-permute-start.7
  32.1 7.8 %copy-start.4 = (f32[32,16,128]{2,1,0:T(8,128)}, f32[32,16,128]{2,1,0:T(8,128)S(1)}, u32[]{:S(2)}) copy-start(f32[32,16,128]{2,1,0:T(8,128)S(1)} %get-tuple-element.897) | copy-start | bytes 786436
  32.1 7.8 %copy-start.6 = (f32[32,16,128]{2,1,0:T(8,128)}, f32[32,16,128]{2,1,0:T(8,128)S(1)}, u32[]{:S(2)}) copy-start(f32[32,16,128]{2,1,0:T(8,128)S(1)} %get-tuple-element.898) | copy-start | bytes 786436
  36.5 3.4 copy-start.10
  39.9 73.0 %all-to-all-start = ((f32[3,3,32,16,128]{4,3,1,0,2:T(8,128)}), f32[3,3,32,16,128]{4,3,1,0,2:T(8,128)S(1)}, u32[]{:S(2)}, u32[]{:S(2)}) async-start(f32[3,3,32,16,128]{4,3,1,0,2:T(8,128)} %pad_maximum_fusion.1), calls=%async_computation | async-start | bytes 4718592 | tf_op jit(solution)/shard_map/all_to_all | solution.py:80
  55.5 28.2 %copy-start.1 = (f32[32,3,4,128,128]{4,0,3,2,1:T(8,128)}, f32[32,3,4,128,128]{4,0,3,2,1:T(8,128)S(1)}, u32[]{:S(2)}) copy-start(f32[32,3,4,128,128]{4,0,3,2,1:T(8,128)S(1)} %convert_multiply_fusion) | copy-start | bytes 75497472
  83.6 25.1 %copy-start.2 = (f32[35,32]{0,1:T(8,128)S(1)}, f32[35,32]{0,1:T(8,128)}, u32[]{:S(2)}) copy-start(f32[35,32]{0,1:T(8,128)} %param.149) | copy-start | bytes 13444
  83.6 27.3 %copy-start.5 = (f32[32,16,128]{2,1,0:T(8,128)S(1)}, f32[32,16,128]{2,1,0:T(8,128)}, u32[]{:S(2)}) copy-start(f32[32,16,128]{2,1,0:T(8,128)} %copy-done.4) | copy-start | bytes 786436
  83.7 27.3 %copy-start.7 = (f32[32,16,128]{2,1,0:T(8,128)S(1)}, f32[32,16,128]{2,1,0:T(8,128)}, u32[]{:S(2)}) copy-start(f32[32,16,128]{2,1,0:T(8,128)} %copy-done.6) | copy-start | bytes 786436
  83.7 27.2 %copy-start.8 = (f32[32,16,128]{2,1,0:T(8,128)S(1)}, f32[32,16,128]{2,1,0:T(8,128)}, u32[]{:S(2)}) copy-start(f32[32,16,128]{2,1,0:T(8,128)} %param.146) | copy-start | bytes 786436
  83.7 27.2 %copy-start.11 = (f32[3,34,1,128]{3,2,0,1:T(1,128)S(1)}, f32[3,34,1,128]{3,2,0,1:T(1,128)}, u32[]{:S(2)}) copy-start(f32[3,34,1,128]{3,2,0,1:T(1,128)} %copy-done.10) | copy-start | bytes 156676
  111.8 468.9 %copy-start.35 = (f32[32]{0:T(128)S(1)}, f32[32]{0:T(128)}, u32[]{:S(2)}) copy-start(f32[32]{0:T(128)} %get-tuple-element.889) | copy-start | bytes 388
  111.8 469.8 %copy-start.30 = (f32[32]{0:T(128)S(1)}, f32[32]{0:T(128)}, u32[]{:S(2)}) copy-start(f32[32]{0:T(128)} %get-tuple-element.888) | copy-start | bytes 388
  111.8 471.3 %copy-start.29 = (f32[32]{0:T(128)S(1)}, f32[32]{0:T(128)}, u32[]{:S(2)}) copy-start(f32[32]{0:T(128)} %get-tuple-element.887) | copy-start | bytes 388
  111.8 473.0 %copy-start.34 = (f32[32]{0:T(128)S(1)}, f32[32]{0:T(128)}, u32[]{:S(2)}) copy-start(f32[32]{0:T(128)} %get-tuple-element.886) | copy-start | bytes 388
  111.8 474.7 %copy-start.28 = (f32[32]{0:T(128)S(1)}, f32[32]{0:T(128)}, u32[]{:S(2)}) copy-start(f32[32]{0:T(128)} %get-tuple-element.885) | copy-start | bytes 388
  111.8 476.3 %copy-start.27 = (f32[32]{0:T(128)S(1)}, f32[32]{0:T(128)}, u32[]{:S(2)}) copy-start(f32[32]{0:T(128)} %get-tuple-element.884) | copy-start | bytes 388
  111.8 478.0 %copy-start.26 = (f32[32]{0:T(128)S(1)}, f32[32]{0:T(128)}, u32[]{:S(2)}) copy-start(f32[32]{0:T(128)} %get-tuple-element.883) | copy-start | bytes 388
  111.8 479.7 %copy-start.25 = (f32[32]{0:T(128)S(1)}, f32[32]{0:T(128)}, u32[]{:S(2)}) copy-start(f32[32]{0:T(128)} %get-tuple-element.882) | copy-start | bytes 388
  111.8 481.4 %copy-start.24 = (f32[32]{0:T(128)S(1)}, f32[32]{0:T(128)}, u32[]{:S(2)}) copy-start(f32[32]{0:T(128)} %get-tuple-element.881) | copy-start | bytes 388
  111.9 483.2 %copy-start.23 = (f32[32]{0:T(128)S(1)}, f32[32]{0:T(128)}, u32[]{:S(2)}) copy-start(f32[32]{0:T(128)} %get-tuple-element.880) | copy-start | bytes 388
  111.9 484.8 %copy-start.22 = (f32[32]{0:T(128)S(1)}, f32[32]{0:T(128)}, u32[]{:S(2)}) copy-start(f32[32]{0:T(128)} %get-tuple-element.879) | copy-start | bytes 388
  111.9 486.5 %copy-start.33 = (f32[32]{0:T(128)S(1)}, f32[32]{0:T(128)}, u32[]{:S(2)}) copy-start(f32[32]{0:T(128)} %get-tuple-element.878) | copy-start | bytes 388
  111.9 488.2 %copy-start.21 = (f32[32]{0:T(128)S(1)}, f32[32]{0:T(128)}, u32[]{:S(2)}) copy-start(f32[32]{0:T(128)} %get-tuple-element.877) | copy-start | bytes 388
  111.9 489.8 %copy-start.20 = (f32[32]{0:T(128)S(1)}, f32[32]{0:T(128)}, u32[]{:S(2)}) copy-start(f32[32]{0:T(128)} %get-tuple-element.876) | copy-start | bytes 388
  111.9 491.5 %copy-start.19 = (f32[32]{0:T(128)S(1)}, f32[32]{0:T(128)}, u32[]{:S(2)}) copy-start(f32[32]{0:T(128)} %get-tuple-element.875) | copy-start | bytes 388
  111.9 493.2 %copy-start.18 = (f32[32]{0:T(128)S(1)}, f32[32]{0:T(128)}, u32[]{:S(2)}) copy-start(f32[32]{0:T(128)} %get-tuple-element.873) | copy-start | bytes 388
  111.9 494.9 %copy-start.17 = (f32[32]{0:T(128)S(1)}, f32[32]{0:T(128)}, u32[]{:S(2)}) copy-start(f32[32]{0:T(128)} %get-tuple-element.872) | copy-start | bytes 388
  111.9 496.5 %copy-start.16 = (f32[32]{0:T(128)S(1)}, f32[32]{0:T(128)}, u32[]{:S(2)}) copy-start(f32[32]{0:T(128)} %get-tuple-element.871) | copy-start | bytes 388
  111.9 498.2 %copy-start.15 = (f32[32]{0:T(128)S(1)}, f32[32]{0:T(128)}, u32[]{:S(2)}) copy-start(f32[32]{0:T(128)} %get-tuple-element.870) | copy-start | bytes 388
  112.0 499.9 %copy-start.32 = (f32[32]{0:T(128)S(1)}, f32[32]{0:T(128)}, u32[]{:S(2)}) copy-start(f32[32]{0:T(128)} %get-tuple-element.869) | copy-start | bytes 388
  112.0 501.5 %copy-start.14 = (f32[32]{0:T(128)S(1)}, f32[32]{0:T(128)}, u32[]{:S(2)}) copy-start(f32[32]{0:T(128)} %get-tuple-element.868) | copy-start | bytes 388
  112.0 503.2 %copy-start.13 = (f32[32]{0:T(128)S(1)}, f32[32]{0:T(128)}, u32[]{:S(2)}) copy-start(f32[32]{0:T(128)} %get-tuple-element.867) | copy-start | bytes 388
  112.0 504.8 %copy-start.12 = (f32[32]{0:T(128)S(1)}, f32[32]{0:T(128)}, u32[]{:S(2)}) copy-start(f32[32]{0:T(128)} %get-tuple-element.866) | copy-start | bytes 388
  112.0 513.4 %copy-start.31 = (f32[32]{0:T(128)S(1)}, f32[32]{0:T(128)}, u32[]{:S(2)}) copy-start(f32[32]{0:T(128)} %get-tuple-element.861) | copy-start | bytes 388
  113.0 1.4 copy-start.3
  498.9 2.1 copy-start.9
  578.6 4.4 copy-start
